TPU v7x, 32 devices: a whole 2x2x4 slice. The times are simulated.
32 devices in a mesh: rep: 8 (over y, x, core), own: 4 (over z).
Axes of the slice: x: 2, y: 2, z: 4, core: 2. Of those that a mesh axis runs over, the one named last changes fastest.
Arguments:
- gradients: bfloat16 [8, 4, 4, 256, 256], P('rep', 'own')
- owner_index: int32 [4], replicated, may hold values from 0 to 3, as said below
- left_stats: float32 [8, 256, 256], P('own'), as said below
- right_stats: float32 [8, 256, 256], P('own'), as said below
- left_roots: bfloat16 [8, 256, 256], P('own'), as said below
- right_roots: bfloat16 [8, 256, 256], P('own'), as said below
- first_moment: float32 [8, 256, 256], P('own')
- second_moment: float32 [8, 256, 256], P('own'), may hold values from 0.05 to 5
- master: float32 [8, 256, 256], P('own'), may hold values from -6 to 6
Outputs:
- new_left: float32 [8, 256, 256], P('own')
- new_right: float32 [8, 256, 256], P('own')
- new_first: float32 [8, 256, 256], P('own')
- new_second: float32 [8, 256, 256], P('own')
- weights: bfloat16 [4, 256, 256], P(None, 'rep')
Inputs may be any that keep to these rules, and one draw needn't show every extreme that they name: `owner_index`: exactly one owner holds 2 blocks, exactly one holds none, every other holds one. `left_stats`: each matrix is symmetric; every diagonal entry exceeds the sum of the magnitudes of the other entries of its row. `right_stats`: each matrix is symmetric; every diagonal entry exceeds the sum of the magnitudes of the other entries of its row. `left_roots`: each matrix is symmetric. `right_roots`: each matrix is symmetric.
All inputs are finite; a program needn't handle non-finite values.
Results may differ from a plain program's by a relative error of at most 0.001.
Values may be sent and summed in bfloat16 or wider, within the bound.
A program may use at most 64 MiB of HBM per device.

v0:
```python
import jax
import jax.numpy as jnp
from jax import lax
from jax.sharding import PartitionSpec as P

NEWTON = 4


stat_decay = 0.95
first_decay = 0.9
second_decay = 0.99
learning_rate = 0.5


def product(first_factor, second_factor):
    return jnp.matmul(first_factor, second_factor, precision=lax.Precision.HIGHEST)


def destinations(owner_index, capacity):
    block_count = owner_index.shape[0]
    positions = jnp.arange(block_count, dtype=jnp.int32)
    same_owner = owner_index[:, None] == owner_index[None, :]
    earlier = positions[None, :] < positions[:, None]
    ranking = jnp.sum((same_owner & earlier).astype(jnp.int32), axis=1)
    return owner_index * capacity + ranking


def inverse_root(statistic, initial):
    current = initial
    for iteration in range(NEWTON):
        square = product(current, current)
        fourth = product(square, square)
        residual = product(fourth, statistic)
        current = (5.0 * current - product(current, residual)) / 4.0
    return current


def local(
    gradients,
    owner_index,
    left_stats,
    right_stats,
    left_roots,
    right_roots,
    first_moment,
    second_moment,
    master,
):
    capacity = left_stats.shape[0]
    block_size = left_stats.shape[-1]
    block_count = owner_index.shape[0]
    owner_count = lax.axis_size("own")
    slot_total = owner_count * capacity
    destination = destinations(owner_index, capacity)
    placement = destination[None, :] == jnp.arange(slot_total, dtype=jnp.int32)[:, None]
    occupied = jnp.any(placement, axis=1)
    source_block = jnp.sum(
        placement.astype(jnp.int32) * jnp.arange(block_count, dtype=jnp.int32)[None, :], axis=1
    )
    local_blocks = gradients.reshape(block_count, block_size, block_size)
    own_position = lax.axis_index("own")
    occupied_here = lax.dynamic_slice_in_dim(occupied, own_position * capacity, capacity)
    slot_terms = jnp.where(
        occupied[:, None, None], local_blocks[source_block].astype(jnp.float32), 0.0
    )
    owned_partial = lax.psum_scatter(slot_terms, "own", scatter_dimension=0, tiled=True)
    summed = lax.psum(owned_partial, "rep")
    transposed = jnp.swapaxes(summed, 1, 2)
    left_new = stat_decay * left_stats + (1.0 - stat_decay) / block_size * product(
        summed, transposed
    )
    right_new = stat_decay * right_stats + (1.0 - stat_decay) / block_size * product(
        transposed, summed
    )
    statistics = jnp.concatenate([left_new, right_new], axis=0)
    starting = jnp.concatenate([left_roots, right_roots], axis=0).astype(jnp.float32)
    roots = inverse_root(statistics, starting)
    left_root = roots[:capacity]
    right_root = roots[capacity:]
    first_new = first_decay * first_moment + (1.0 - first_decay) * summed
    second_new = second_decay * second_moment + (1.0 - second_decay) * summed * summed
    adam_step = first_new / (jnp.sqrt(second_new) + 1e-08)
    precond = product(product(left_root, summed), right_root)
    graft = jnp.sqrt(jnp.sum(adam_step * adam_step, axis=(1, 2))) / (
        jnp.sqrt(jnp.sum(precond * precond, axis=(1, 2))) + 1e-06
    )
    updated = (master - learning_rate * graft[:, None, None] * precond).astype(jnp.bfloat16)
    row_count = block_size // lax.axis_size("rep")
    row_piece = lax.dynamic_slice_in_dim(updated, lax.axis_index("rep") * row_count, row_count, 1)
    gathered = lax.all_gather(row_piece, "own", axis=0, tiled=True)
    weights = gathered[destination]
    keep_slot = occupied_here[:, None, None]
    new_left = jnp.where(keep_slot, left_new, left_stats)
    new_right = jnp.where(keep_slot, right_new, right_stats)
    new_first = jnp.where(keep_slot, first_new, first_moment)
    new_second = jnp.where(keep_slot, second_new, second_moment)
    return (new_left, new_right, new_first, new_second, weights)


def solution(mesh):
    return jax.shard_map(
        local,
        mesh=mesh,
        in_specs=(
            P("rep", "own", None, None, None),
            P(),
            P("own", None, None),
            P("own", None, None),
            P("own", None, None),
            P("own", None, None),
            P("own", None, None),
            P("own", None, None),
            P("own", None, None),
        ),
        out_specs=(
            P("own", None, None),
            P("own", None, None),
            P("own", None, None),
            P("own", None, None),
            P(None, "rep", None),
        ),
        check_vma=False,
    )
```

profile of v0, /device:TPU:0, one launch (start us, length us, event | category | flops | bytes accessed | tf_op | source)
XLA Modules:
  0.0 161.0 jit_solution(4762941962667526766)
XLA Ops:
  7.2 0.9 convert_reduce_fusion
  8.1 0.7 compare_select_fusion
  8.8 0.1 fusion.28
  8.9 0.1 select_reduce_fusion
  9.0 0.6 gather_fusion
  9.6 1.6 %convert_select_fusion = f32[8,256,256]{2,1,0:T(8,128)} fusion(bf16[8,256,256]{2,1,0:T(8,128)(2,1)S(1)} %gather_fusion, pred[8]{0:T(512)(128)(4,1)S(1)} %fusion.28), kind=kLoop, calls=%fused_computation.2 | loop fusion | flops 1048576 | bytes 3145736 | tf_op jit(solution)/shard_map/jit(_where)/select_n | solution.py:63
  11.4 0.8 copy-done.6
  12.2 0.3 fusion.42
  12.5 45.3 %reduce-scatter.2.cloned.1.call-done = f32[2,256,256]{2,1,0:T(8,128)} async-done(((f32[8,256,256]{2,1,0:T(8,128)}), f32[2,256,256]{2,1,0:T(8,128)}) %reduce-scatter.2.cloned.1.call-update) | async-done | bytes 524304 | tf_op jit(solution)/shard_map/reduce_scatter | solution.py:66
  57.8 1.1 fusion.43
  59.0 56.0 %all-reduce.2.cloned.1.call-done = f32[2,256,256]{2,1,0:T(8,128)} async-done(((f32[2,256,256]{2,1,0:T(8,128)}), f32[2,256,256]{2,1,0:T(8,128)}) %all-reduce.2.cloned.1.call-update) | async-done | bytes 524304 | tf_op jit(solution)/shard_map/psum | solution.py:67
  114.9 2.1 %fusion.2 = f32[2,256,256]{2,1,0:T(8,128)S(1)} fusion(f32[2,256,256]{2,1,0:T(8,128)} %all-reduce.2.cloned.1.call-done, f32[2,256,256]{2,1,0:T(8,128)} %param.11), kind=kOutput, calls=%fused_computation.11 | convolution fusion | flops 403046400 | bytes 1572864 | tf_op jit(solution)/shard_map/dot_general | solution.py:16
  117.1 3.7 %multiply_reduce_fusion.1 = (f32[2]{0:T(128)S(1)}, f32[2,256,256]{2,1,0:T(8,128)}, f32[2,256,256]{2,1,0:T(8,128)}, f32[2,256,256]{2,1,0:T(8,128)}, f32[2,256,256]{2,1,0:T(8,128)}, /*index=5*/f32[2,256,256]{2,1,0:T(8,128)S(1)}) fusion(f32[2,256,256]{2,1,0:T(8,128)S(1)} %copy-done.1, f32[2,256,256]{2,1,0:T(8,128)S(1)} %copy-done.3, ...), kind=kOutput, calls=%fused_computation.33 | convolution fusion | flops 405012480 | bytes 5767178 | tf_op jit(solution)/shard_map/dot_general | solution.py:16
  120.8 1.1 fusion.24
  122.0 0.7 convolution_subtract_fusion.3
  122.7 1.2 fusion.10
  123.9 1.1 fusion.44
  125.1 1.1 fusion.23
  126.3 1.2 convolution_subtract_fusion.2
  127.5 1.2 fusion.7
  128.7 1.3 fusion.45
  130.0 1.1 fusion.22
  131.2 1.2 convolution_subtract_fusion.1
  132.4 1.2 fusion.4
  133.6 1.1 fusion.46
  134.8 1.1 fusion.21
  135.9 1.3 fusion
  137.2 0.7 fusion.47
  137.9 0.8 multiply_reduce_fusion
  138.7 0.9 fusion.27
  139.6 13.3 %all_gather.3 = bf16[8,32,256]{2,1,0:T(8,128)(2,1)S(1)} all-gather(bf16[2,32,256]{2,1,0:T(8,128)(2,1)S(1)} %fusion.27), channel_id=1, replica_groups=mesh['rep'=8,'own'=4] {'own'}, dimensions={0}, use_global_device_ids=true | all-gather | bytes 163840 | tf_op jit(solution)/shard_map/all_gather | solution.py:90
  152.9 1.2 gather_fusion.1
  (24 shorter events, 0.3 us)
Async XLA Ops:
  7.2 1.8 %copy-start = (bf16[1,1,4,256,256]{4,3,2,1,0:T(8,128)(2,1)S(1)}, bf16[1,1,4,256,256]{4,3,2,1,0:T(8,128)(2,1)}, u32[]{:S(2)}) copy-start(bf16[1,1,4,256,256]{4,3,2,1,0:T(8,128)(2,1)} %param.9) | copy-start | bytes 1572868
  7.2 50.6 %reduce-scatter.2.cloned.1.call-start = ((), (), s32[]{:S(2)}) async-start(), calls=%async_computation.1 | async-start | bytes 2621440 | tf_op jit(solution)/shard_map/reduce_scatter | solution.py:66
  9.6 1.8 %copy-start.5 = (bf16[2,256,256]{2,1,0:T(8,128)(2,1)S(1)}, bf16[2,256,256]{2,1,0:T(8,128)(2,1)}, u32[]{:S(2)}) copy-start(bf16[2,256,256]{2,1,0:T(8,128)(2,1)} %param.13) | copy-start | bytes 786436
  11.2 0.9 copy-start.6
  11.3 103.7 %all-reduce.2.cloned.1.call-start = ((), (), s32[]{:S(2)}) async-start(), calls=%async_computation.2 | async-start | bytes 1048576 | tf_op jit(solution)/shard_map/psum | solution.py:67
  58.9 58.2 %copy-start.2 = (f32[2,256,256]{2,1,0:T(8,128)S(1)}, f32[2,256,256]{2,1,0:T(8,128)}, u32[]{:S(2)}) copy-start(f32[2,256,256]{2,1,0:T(8,128)} %param.11) | copy-start | bytes 1572868
  59.0 58.2 %copy-start.3 = (f32[2,256,256]{2,1,0:T(8,128)S(1)}, f32[2,256,256]{2,1,0:T(8,128)}, u32[]{:S(2)}) copy-start(f32[2,256,256]{2,1,0:T(8,128)} %param.15) | copy-start | bytes 1572868
  114.9 2.2 %copy-start.1 = (f32[2,256,256]{2,1,0:T(8,128)S(1)}, f32[2,256,256]{2,1,0:T(8,128)}, u32[]{:S(2)}) copy-start(f32[2,256,256]{2,1,0:T(8,128)} %all-reduce.2.cloned.1.call-done) | copy-start | bytes 1572868
  114.9 2.2 %copy-start.4 = (f32[2,256,256]{2,1,0:T(8,128)S(1)}, f32[2,256,256]{2,1,0:T(8,128)}, u32[]{:S(2)}) copy-start(f32[2,256,256]{2,1,0:T(8,128)} %param.16) | copy-start | bytes 1572868
Sparse Core Ops, SparseCore 0:
  11.4 46.3 reduce-scatter.1
  60.9 54.0 all-reduce.1
where the time goes:
time: 161 us
  waiting for transfers between devices  101 us (63%)
  matrix products  25 us (16%)
  between operations  14.3 us (9%)
  blocking collectives  13.3 us (8%)
  other arithmetic  4.32 us (3%)
  local copies, waits for them, and re-layouts  2.7 us (2%)
    psum x1, waiting for transfers between devices, local(): summed = lax.psum(owned_partial, 'rep')  56 us
    reduce_scatter x1, waiting for transfers between devices, local(): lax.psum_scatter(slot_terms, 'own', scatter_dimension=0, tiled=True)  45.3 us
    dot_general x20, matrix products, product(): jnp.matmul(first_factor, second_factor, precision=lax.Precision.HIGHEST)  25 us
    all_gather x1, blocking collectives, local(): gathered = lax.all_gather(row_piece, 'own', axis=0, tiled=True)  13.3 us
  transfers between devices with their start and end apart: 2, of which 2 were waited for; matrix products, arithmetic and copies ran while one was open for 1% of the time, Pallas kernels for 0%

commit v1 on v0

v1 whole, which is shorter than its diff:
```python
import functools

import jax
import jax.numpy as jnp
from jax import lax
from jax.experimental import pallas as pl
from jax.experimental.pallas import tpu as pltpu
from jax.sharding import PartitionSpec as P

NEWTON = 4


stat_decay = 0.95
first_decay = 0.9
second_decay = 0.99
learning_rate = 0.5


def slot_of(owner_ref, block, capacity):
    rank = jnp.int32(0)
    for earlier in range(block):
        rank = rank + jnp.where(owner_ref[earlier] == owner_ref[block], 1, 0)
    return owner_ref[block] * capacity + rank


def send(source, target, send_sem, recv_sem, device):
    copy = pltpu.make_async_remote_copy(
        src_ref=source,
        dst_ref=target,
        send_sem=send_sem,
        recv_sem=recv_sem,
        device_id=device,
        device_id_type=pl.DeviceIdType.MESH,
    )
    copy.start()
    return copy


def greet(devices):
    barrier = pltpu.get_barrier_semaphore()
    for device in devices:
        pl.semaphore_signal(
            barrier, inc=1, device_id=device, device_id_type=pl.DeviceIdType.MESH
        )
    pl.semaphore_wait(barrier, len(devices))


def exchange(
    reps,
    owns,
    owner_ref,
    gradients_ref,
    summed_ref,
    raw,
    partial,
    arrived,
    same,
    other,
    local_sem,
    raw_send,
    raw_recv,
    own_send,
    own_recv,
    same_send,
    same_recv,
    other_send,
    other_recv,
):
    rep = lax.axis_index("rep")
    own = lax.axis_index("own")
    block_count = owner_ref.shape[0]
    capacity = summed_ref.shape[0]
    half = reps // 2

    def rep_device(target):
        return (target, own)

    def own_device(target):
        return (rep, target)

    mine = pltpu.make_async_copy(gradients_ref.at[:, rep], raw.at[0], local_sem)
    mine.start()
    greet(
        [rep_device(lax.rem(rep + step, reps)) for step in range(1, reps)]
        + [own_device(lax.rem(own + step, owns)) for step in range(1, owns)]
    )
    copies = []
    for step in range(1, reps):
        target = lax.rem(rep + step, reps)
        copies.append(
            send(
                gradients_ref.at[:, target],
                raw.at[step],
                raw_send.at[step],
                raw_recv.at[step],
                rep_device(target),
            )
        )
    slots = [slot_of(owner_ref, block, capacity) for block in range(block_count)]

    def source(slot):
        found = jnp.int32(0)
        for block in range(block_count):
            found = found + jnp.where(slots[block] == slot, block, 0)
        return found

    mine.wait()
    for copy in copies:
        copy.wait()

    copies = []
    for step in [*range(1, owns), 0]:
        target = lax.rem(own + step, owns)
        for place in range(capacity):
            block = source(target * capacity + place)
            total = raw[0, block].astype(jnp.float32)
            for peer in range(1, reps):
                total = total + raw[peer, block].astype(jnp.float32)
            partial[step, place] = total
        if step:
            copies.append(
                send(
                    partial.at[step],
                    arrived.at[step],
                    own_send.at[step],
                    own_recv.at[step],
                    own_device(target),
                )
            )
    for copy in copies:
        copy.wait()
    total = partial[0]
    for step in range(1, owns):
        total = total + arrived[step]
    same[0] = total

    high = lax.div(rep, 2)
    low = lax.rem(rep, 2)
    partner = rep_device(rep + 1 - 2 * low)
    first = []
    for step in range(1, half):
        target = lax.rem(high + step, half) * 2 + low
        first.append(
            send(
                same.at[0],
                same.at[step],
                same_send.at[step],
                same_recv.at[step],
                rep_device(target),
            )
        )
    second = [send(same.at[0], other.at[0], other_send.at[0], other_recv.at[0], partner)]
    for step in range(1, half):
        first[step - 1].wait_recv()
        second.append(
            send(
                same.at[step],
                other.at[step],
                other_send.at[step],
                other_recv.at[step],
                partner,
            )
        )
    for step in range(half):
        origin = lax.rem(high + half - step, half) * 2
        summed_ref[:, origin + low] = same[step]
        second[step].wait_recv()
        summed_ref[:, origin + 1 - low] = other[step]
    for copy in first + second:
        copy.wait_send()


def parts(value):
    upper = value.astype(jnp.bfloat16)
    lower = (value - upper.astype(jnp.float32)).astype(jnp.bfloat16)
    return upper, lower


def multiply(first, second, first_axis=1, second_axis=0):
    def dot(a, b):
        return lax.dot_general(
            a,
            b,
            (((first_axis,), (second_axis,)), ((), ())),
            preferred_element_type=jnp.float32,
        )

    return dot(first[0], second[0]) + (dot(first[0], second[1]) + dot(first[1], second[0]))


def refresh(
    row_count,
    owner_ref,
    summed_ref,
    left_ref,
    right_ref,
    left_root_ref,
    right_root_ref,
    first_ref,
    second_ref,
    master_ref,
    new_left_ref,
    new_right_ref,
    new_first_ref,
    new_second_ref,
    rows_ref,
    statistic,
    current,
    kept,
):
    capacity = left_ref.shape[0]
    block_size = left_ref.shape[-1]
    block_count = owner_ref.shape[0]
    rep = lax.axis_index("rep")
    own = lax.axis_index("own")
    slots = [slot_of(owner_ref, block, capacity) for block in range(block_count)]
    scale = (1.0 - stat_decay) / block_size

    for place in range(capacity):
        split = parts(summed_ref[place])
        statistic[place] = stat_decay * left_ref[place] + scale * multiply(split, split, 1, 1)
        statistic[capacity + place] = stat_decay * right_ref[place] + scale * multiply(
            split, split, 0, 0
        )
        current[place] = left_root_ref[place].astype(jnp.float32)
        current[capacity + place] = right_root_ref[place].astype(jnp.float32)

    chains = range(2 * capacity)

    def newton(iteration, carry):
        roots = [parts(current[chain]) for chain in chains]
        squares = [parts(multiply(roots[chain], roots[chain])) for chain in chains]
        fourths = [parts(multiply(squares[chain], squares[chain])) for chain in chains]
        residuals = [
            parts(multiply(fourths[chain], parts(statistic[chain]))) for chain in chains
        ]
        for chain in chains:
            current[chain] = (
                5.0 * current[chain] - multiply(roots[chain], residuals[chain])
            ) / 4.0
        return carry

    lax.fori_loop(0, NEWTON, newton, 0)

    def total(value):
        return jnp.sum(jnp.sum(value, axis=0, keepdims=True), axis=1, keepdims=True)

    for place in range(capacity):
        slot = own * capacity + place
        held = jnp.int32(0)
        for block in range(block_count):
            held = held + jnp.where(slots[block] == slot, 1, 0)
        summed = summed_ref[place]
        precond = multiply(
            parts(multiply(parts(current[place]), parts(summed))),
            parts(current[capacity + place]),
        )
        first_new = first_decay * first_ref[place] + (1.0 - first_decay) * summed
        second_new = second_decay * second_ref[place] + (1.0 - second_decay) * summed * summed
        adam_step = first_new / (jnp.sqrt(second_new) + 1e-08)
        graft = jnp.sqrt(total(adam_step * adam_step)) / (
            jnp.sqrt(total(precond * precond)) + 1e-06
        )
        kept[...] = precond
        start = pl.multiple_of(rep * row_count, row_count)
        rows = pl.ds(start, row_count)
        rows_ref[place] = (
            master_ref[place, rows, :] - learning_rate * graft * kept[rows, :]
        ).astype(jnp.bfloat16)

        @pl.when(held > 0)
        def _():
            new_left_ref[place] = statistic[place]
            new_right_ref[place] = statistic[capacity + place]
            new_first_ref[place] = first_new
            new_second_ref[place] = second_new

        @pl.when(held == 0)
        def _():
            new_left_ref[place] = left_ref[place]
            new_right_ref[place] = right_ref[place]
            new_first_ref[place] = first_ref[place]
            new_second_ref[place] = second_ref[place]


def share(owns, owner_ref, rows_ref, weights_ref, gathered, send_sem, recv_sem):
    rep = lax.axis_index("rep")
    own = lax.axis_index("own")
    block_count = owner_ref.shape[0]
    capacity = rows_ref.shape[0]
    targets = [(rep, lax.rem(own + step, owns)) for step in range(1, owns)]
    greet(targets)
    copies = [
        send(
            rows_ref,
            gathered.at[pl.ds(step * capacity, capacity)],
            send_sem.at[step],
            recv_sem.at[step],
            targets[step - 1],
        )
        for step in range(1, owns)
    ]
    gathered[0:capacity] = rows_ref[...]
    for copy in copies:
        copy.wait()
    for block in range(block_count):
        slot = slot_of(owner_ref, block, capacity)
        step = lax.rem(own + owns - owner_ref[block], owns)
        place = jnp.minimum(slot - owner_ref[block] * capacity, capacity - 1)
        weights_ref[block] = gathered[step * capacity + place]


def local(
    reps,
    owns,
    gradients,
    owner_index,
    left_stats,
    right_stats,
    left_roots,
    right_roots,
    first_moment,
    second_moment,
    master,
):
    capacity = left_stats.shape[0]
    block_size = left_stats.shape[-1]
    block_count = owner_index.shape[0]
    row_count = block_size // reps
    half = reps // 2
    vmem = pl.BlockSpec(memory_space=pltpu.VMEM)
    smem = pl.BlockSpec(memory_space=pltpu.SMEM)
    dma = pltpu.SemaphoreType.DMA
    piece = (capacity, row_count, block_size)

    summed = pl.pallas_call(
        functools.partial(exchange, reps, owns),
        out_shape=jax.ShapeDtypeStruct((capacity, reps, row_count, block_size), jnp.float32),
        in_specs=[smem, pl.BlockSpec(memory_space=pl.ANY)],
        out_specs=vmem,
        scratch_shapes=[
            pltpu.VMEM((reps, block_count, row_count, block_size), jnp.bfloat16),
            pltpu.VMEM((owns, *piece), jnp.float32),
            pltpu.VMEM((owns, *piece), jnp.float32),
            pltpu.VMEM((half, *piece), jnp.float32),
            pltpu.VMEM((half, *piece), jnp.float32),
            dma(()),
            dma((reps,)),
            dma((reps,)),
            dma((owns,)),
            dma((owns,)),
            dma((half,)),
            dma((half,)),
            dma((half,)),
            dma((half,)),
        ],
        compiler_params=pltpu.CompilerParams(
            collective_id=0, has_side_effects=True, vmem_limit_bytes=24 * 2**20
        ),
        name="exchange",
    )(owner_index, gradients.reshape(block_count, reps, row_count, block_size))
    summed = summed.reshape(capacity, block_size, block_size)

    full = jax.ShapeDtypeStruct((capacity, block_size, block_size), jnp.float32)
    new_left, new_right, new_first, new_second, rows = pl.pallas_call(
        functools.partial(refresh, row_count),
        out_shape=(full, full, full, full, jax.ShapeDtypeStruct(piece, jnp.bfloat16)),
        in_specs=[smem] + [vmem] * 8,
        out_specs=(vmem,) * 5,
        scratch_shapes=[
            pltpu.VMEM((2 * capacity, block_size, block_size), jnp.float32),
            pltpu.VMEM((2 * capacity, block_size, block_size), jnp.float32),
            pltpu.VMEM((block_size, block_size), jnp.float32),
        ],
        compiler_params=pltpu.CompilerParams(vmem_limit_bytes=24 * 2**20),
        name="refresh",
    )(
        owner_index,
        summed,
        left_stats,
        right_stats,
        left_roots,
        right_roots,
        first_moment,
        second_moment,
        master,
    )

    weights = pl.pallas_call(
        functools.partial(share, owns),
        out_shape=jax.ShapeDtypeStruct((block_count, row_count, block_size), jnp.bfloat16),
        in_specs=[smem, vmem],
        out_specs=vmem,
        scratch_shapes=[
            pltpu.VMEM((owns * capacity, row_count, block_size), jnp.bfloat16),
            dma((owns,)),
            dma((owns,)),
        ],
        compiler_params=pltpu.CompilerParams(
            collective_id=1, has_side_effects=True, vmem_limit_bytes=8 * 2**20
        ),
        name="share",
    )(owner_index, rows)
    return (new_left, new_right, new_first, new_second, weights)


def solution(mesh):
    return jax.shard_map(
        functools.partial(local, mesh.shape["rep"], mesh.shape["own"]),
        mesh=mesh,
        in_specs=(
            P("rep", "own", None, None, None),
            P(),
            P("own", None, None),
            P("own", None, None),
            P("own", None, None),
            P("own", None, None),
            P("own", None, None),
            P("own", None, None),
            P("own", None, None),
        ),
        out_specs=(
            P("own", None, None),
            P("own", None, None),
            P("own", None, None),
            P("own", None, None),
            P(None, "rep", None),
        ),
        check_vma=False,
    )
```

time: 161 us -> 53 us (0.33)
  waiting for transfers between devices: 101 us -> 0 us
  Pallas kernels: 0 us -> 44.6 us
  matrix products: 25 us -> 0 us
  between operations: 14.3 us -> 0.69 us
  blocking collectives: 13.3 us -> 0 us
  local copies, waits for them, and re-layouts: 2.7 us -> 7.35 us
  other arithmetic: 4.32 us -> 0 us
    psum x1 -> x0, waiting for transfers between devices: 56 us -> none  [local(): summed = lax.psum(owned_partial, 'rep')]
    reduce_scatter x1 -> x0, waiting for transfers between devices: 45.3 us -> none  [local(): lax.psum_scatter(slot_terms, 'own', scatter_dimension=0, tiled=True)]
    pallas_call x0 -> x3, Pallas kernels: none -> 44.6 us  [the longest x1 26 us: local(): pl.pallas_call(functools.partial(exchange, reps, owns), out_shape=jax.Sha...]
    dot_general x20 -> x0, matrix products: 25 us -> none  [product(): jnp.matmul(first_factor, second_factor, precision=lax.Precision.HIGHEST)]
    all_gather x1 -> x0, blocking collectives: 13.3 us -> none  [local(): gathered = lax.all_gather(row_piece, 'own', axis=0, tiled=True)]
    unnamed x15 -> x19, local copies, waits for them, and re-layouts: 0.81 us -> 7.35 us
    select_n x3 -> x0, other arithmetic: 2.28 us -> none  [the longest x1 1.61 us: local(): jnp.where(occupied[:, None, None], local_blocks[source_block].astype(jnp....]
    gather x2 -> x0, local copies, waits for them, and re-layouts: 1.79 us -> none  [the longest x1 1.18 us: local(): weights = gathered[destination]]
  transfers between devices with their start and end apart: 2 -> 0, of which waited for: 2 -> 0; matrix products, arithmetic and copies ran while one was open for 1% -> 0% of each run, Pallas kernels for 0% -> 0%
where the time goes in v1:
time: 53 us; the launch traced here: 52.7 us
  Pallas kernels  44.6 us (84%)
  local copies, waits for them, and re-layouts  7.35 us (14%)
  between operations  0.69 us (1%)
    pallas_call x1, Pallas kernels, local(): pl.pallas_call(functools.partial(exchange, reps, owns), out_shape=jax.Sha...  26 us
    pallas_call x1, Pallas kernels, local(): pl.pallas_call(functools.partial(refresh, row_count), out_shape=(full, fu...  11.3 us
    unnamed x19, local copies, waits for them, and re-layouts  7.35 us
    pallas_call x1, Pallas kernels, local(): pl.pallas_call(functools.partial(share, owns), out_shape=jax.ShapeDtypeSt...  7.32 us

profile of v1, /device:TPU:0, one launch (start us, length us, event | category | flops | bytes accessed | tf_op | source)
XLA Modules:
  0.0 52.7 jit_solution(11626069660659752806)
XLA Ops:
  0.6 0.0 copy-start.8
  0.6 0.6 %copy-done.8 = s32[4]{0:T(128)S(1)} copy-done((s32[4]{0:T(128)S(1)}, s32[4]{0:T(128)}, u32[]{:S(2)}) %copy-start.8) | copy-done | bytes 40
  1.3 0.0 copy-start
  1.3 1.0 %copy-done = bf16[1,1,4,256,256]{4,3,2,1,0:T(8,128)(2,1)S(1)} copy-done((bf16[1,1,4,256,256]{4,3,2,1,0:T(8,128)(2,1)S(1)}, bf16[1,1,4,256,256]{4,3,2,1,0:T(8,128)(2,1)}, u32[]{:S(2)}) %copy-start) | copy-done | bytes 524312
  2.3 0.0 copy-start.1
  2.3 0.0 copy-start.2
  2.3 26.0 %exchange.1 = f32[2,8,32,256]{3,2,1,0:T(8,128)S(1)} custom-call(s32[4]{0:T(128)S(1)} %copy-done.8, bf16[4,8,32,256]{3,2,1,0:T(8,128)(2,1)S(1)} %bitcast.3), custom_call_target="tpu_custom_call" | custom-call | tf_op jit(solution)/shard_map/exchange/pallas_call | solution.py:336
  28.4 0.0 copy-done.1
  28.4 0.0 copy-done.2
  28.4 0.0 copy-start.3
  28.4 1.0 %copy-done.3 = f32[2,256,256]{2,1,0:T(8,128)S(1)} copy-done((f32[2,256,256]{2,1,0:T(8,128)S(1)}, f32[2,256,256]{2,1,0:T(8,128)}, u32[]{:S(2)}) %copy-start.3) | copy-done | bytes 524312
  29.5 0.0 copy-start.4
  29.5 1.0 %copy-done.4 = f32[2,256,256]{2,1,0:T(8,128)S(1)} copy-done((f32[2,256,256]{2,1,0:T(8,128)S(1)}, f32[2,256,256]{2,1,0:T(8,128)}, u32[]{:S(2)}) %copy-start.4) | copy-done | bytes 524312
  30.5 0.0 copy-start.5
  30.5 1.0 %copy-done.5 = f32[2,256,256]{2,1,0:T(8,128)S(1)} copy-done((f32[2,256,256]{2,1,0:T(8,128)S(1)}, f32[2,256,256]{2,1,0:T(8,128)}, u32[]{:S(2)}) %copy-start.5) | copy-done | bytes 524312
  31.5 0.0 copy-start.6
  31.5 0.9 %copy-done.6 = bf16[2,256,256]{2,1,0:T(8,128)(2,1)S(1)} copy-done((bf16[2,256,256]{2,1,0:T(8,128)(2,1)S(1)}, bf16[2,256,256]{2,1,0:T(8,128)(2,1)}, u32[]{:S(2)}) %copy-start.6) | copy-done | bytes 262168
  32.5 0.0 copy-start.7
  32.5 0.9 %copy-done.7 = bf16[2,256,256]{2,1,0:T(8,128)(2,1)S(1)} copy-done((bf16[2,256,256]{2,1,0:T(8,128)(2,1)S(1)}, bf16[2,256,256]{2,1,0:T(8,128)(2,1)}, u32[]{:S(2)}) %copy-start.7) | copy-done | bytes 262168
  33.4 11.3 %refresh.1 = (f32[2,256,256]{2,1,0:T(8,128)}, f32[2,256,256]{2,1,0:T(8,128)}, f32[2,256,256]{2,1,0:T(8,128)}, f32[2,256,256]{2,1,0:T(8,128)}, bf16[2,32,256]{2,1,0:T(8,128)(2,1)S(1)}) custom-call(s32[4]{0:T(128)S(1)} %copy-done.8, f32[2,256,256]{2,1,0:T(8,128)S(1)} %bitcast.2, f32[2,256,256]{2,1,0:T(8,128)S(1)} %copy-done.1, f32[2,256,256]{2,1,0:T(8,128)S(1)} %copy-done.2, ...), custom_call_target="tpu_custom_call" | custom-call | tf_op jit(solution)/shard_map/refresh/pallas_call | solution.py:365
  44.7 7.3 %share.1 = bf16[4,32,256]{2,1,0:T(8,128)(2,1)S(1)} custom-call(s32[4]{0:T(128)S(1)} %copy-done.8, bf16[2,32,256]{2,1,0:T(8,128)(2,1)S(1)} %get-tuple-element.14.rows_ref), custom_call_target="tpu_custom_call" | custom-call | tf_op jit(solution)/shard_map/share/pallas_call | solution.py:389
  52.0 0.6 %copy.15 = bf16[4,32,256]{2,1,0:T(8,128)(2,1)} copy(bf16[4,32,256]{2,1,0:T(8,128)(2,1)S(1)} %share.1) | data formatting | bytes 131072
Async XLA Ops:
  0.6 0.7 %copy-start.8 = (s32[4]{0:T(128)S(1)}, s32[4]{0:T(128)}, u32[]{:S(2)}) copy-start(s32[4]{0:T(128)} %owner_ref.5) | copy-start | bytes 52
  1.3 1.0 %copy-start = (bf16[1,1,4,256,256]{4,3,2,1,0:T(8,128)(2,1)S(1)}, bf16[1,1,4,256,256]{4,3,2,1,0:T(8,128)(2,1)}, u32[]{:S(2)}) copy-start(bf16[1,1,4,256,256]{4,3,2,1,0:T(8,128)(2,1)} %param.9) | copy-start | bytes 1572868
  2.3 26.1 %copy-start.1 = (f32[2,256,256]{2,1,0:T(8,128)S(1)}, f32[2,256,256]{2,1,0:T(8,128)}, u32[]{:S(2)}) copy-start(f32[2,256,256]{2,1,0:T(8,128)} %left_ref.1) | copy-start | bytes 1572868
  2.3 26.1 %copy-start.2 = (f32[2,256,256]{2,1,0:T(8,128)S(1)}, f32[2,256,256]{2,1,0:T(8,128)}, u32[]{:S(2)}) copy-start(f32[2,256,256]{2,1,0:T(8,128)} %right_ref.1) | copy-start | bytes 1572868
  28.4 1.0 %copy-start.3 = (f32[2,256,256]{2,1,0:T(8,128)S(1)}, f32[2,256,256]{2,1,0:T(8,128)}, u32[]{:S(2)}) copy-start(f32[2,256,256]{2,1,0:T(8,128)} %first_ref.1) | copy-start | bytes 1572868
  29.5 1.0 %copy-start.4 = (f32[2,256,256]{2,1,0:T(8,128)S(1)}, f32[2,256,256]{2,1,0:T(8,128)}, u32[]{:S(2)}) copy-start(f32[2,256,256]{2,1,0:T(8,128)} %second_ref.1) | copy-start | bytes 1572868
  30.5 1.0 %copy-start.5 = (f32[2,256,256]{2,1,0:T(8,128)S(1)}, f32[2,256,256]{2,1,0:T(8,128)}, u32[]{:S(2)}) copy-start(f32[2,256,256]{2,1,0:T(8,128)} %master_ref.1) | copy-start | bytes 1572868
  31.5 0.9 %copy-start.6 = (bf16[2,256,256]{2,1,0:T(8,128)(2,1)S(1)}, bf16[2,256,256]{2,1,0:T(8,128)(2,1)}, u32[]{:S(2)}) copy-start(bf16[2,256,256]{2,1,0:T(8,128)(2,1)} %left_root_ref.1) | copy-start | bytes 786436
  32.5 0.9 %copy-start.7 = (bf16[2,256,256]{2,1,0:T(8,128)(2,1)S(1)}, bf16[2,256,256]{2,1,0:T(8,128)(2,1)}, u32[]{:S(2)}) copy-start(bf16[2,256,256]{2,1,0:T(8,128)(2,1)} %right_root_ref.1) | copy-start | bytes 786436

commit v2 on v0

v2 whole, which is shorter than its diff:
```python
import functools

import jax
import jax.numpy as jnp
from jax import lax
from jax.experimental import pallas as pl
from jax.experimental.pallas import tpu as pltpu
from jax.sharding import PartitionSpec as P

NEWTON = 4


stat_decay = 0.95
first_decay = 0.9
second_decay = 0.99
learning_rate = 0.5


def slot_of(owner_ref, block, capacity):
    rank = jnp.int32(0)
    for earlier in range(block):
        rank = rank + jnp.where(owner_ref[earlier] == owner_ref[block], 1, 0)
    return owner_ref[block] * capacity + rank


def send(source, target, send_sem, recv_sem, device):
    copy = pltpu.make_async_remote_copy(
        src_ref=source,
        dst_ref=target,
        send_sem=send_sem,
        recv_sem=recv_sem,
        device_id=device,
        device_id_type=pl.DeviceIdType.MESH,
    )
    copy.start()
    return copy


def greet(devices):
    barrier = pltpu.get_barrier_semaphore()
    for device in devices:
        pl.semaphore_signal(
            barrier, inc=1, device_id=device, device_id_type=pl.DeviceIdType.MESH
        )
    pl.semaphore_wait(barrier, len(devices))


def dot(first, second, first_axis=1, second_axis=0):
    return lax.dot_general(
        first,
        second,
        (((first_axis,), (second_axis,)), ((), ())),
        preferred_element_type=jnp.float32,
    )


def parts(value):
    upper = value.astype(jnp.bfloat16)
    lower = (value - upper.astype(jnp.float32)).astype(jnp.bfloat16)
    return upper, lower


def multiply(first, second, first_axis=1, second_axis=0):
    return dot(first[0], second[0], first_axis, second_axis) + (
        dot(first[0], second[1], first_axis, second_axis)
        + dot(first[1], second[0], first_axis, second_axis)
    )


def total(value):
    return jnp.sum(jnp.sum(value, axis=0, keepdims=True), axis=1, keepdims=True)


def step_kernel(
    reps,
    owns,
    chunks,
    owner_ref,
    gradients_ref,
    left_ref,
    right_ref,
    left_root_ref,
    right_root_ref,
    first_ref,
    second_ref,
    master_ref,
    new_left_ref,
    new_right_ref,
    new_first_ref,
    new_second_ref,
    weights_ref,
    raw,
    partial,
    arrived,
    same,
    other,
    summed,
    roots,
    statistics,
    first_in,
    second_in,
    master_in,
    fourth,
    upper,
    lower,
    current,
    kept,
    outgoing,
    gathered,
    load_sem,
    store_sem,
    mine_sem,
    raw_send,
    raw_recv,
    own_send,
    own_recv,
    same_send,
    same_recv,
    other_send,
    other_recv,
    row_send,
    row_recv,
):
    rep = lax.axis_index("rep")
    own = lax.axis_index("own")
    block_count = owner_ref.shape[0]
    capacity = new_left_ref.shape[0]
    block_size = new_left_ref.shape[-1]
    row_count = weights_ref.shape[1]
    piece_rows = row_count // chunks
    half = reps // 2
    chains = range(2 * capacity)

    def rep_device(target):
        return (target, own)

    def own_device(target):
        return (rep, target)

    loads = []
    for place, (source_ref, target_ref) in enumerate(
        (
            (left_root_ref, roots.at[0:capacity]),
            (right_root_ref, roots.at[capacity : 2 * capacity]),
            (left_ref, statistics.at[0:capacity]),
            (right_ref, statistics.at[capacity : 2 * capacity]),
            (first_ref, first_in),
            (second_ref, second_in),
            (master_ref, master_in),
        )
    ):
        loads.append(pltpu.make_async_copy(source_ref, target_ref, load_sem.at[place]))
        loads[-1].start()
    mine = []
    for chunk in range(chunks):
        mine.append(
            pltpu.make_async_copy(
                gradients_ref.at[:, rep * chunks + chunk], raw[chunk].at[0], mine_sem.at[chunk]
            )
        )
        mine[-1].start()
    greet(
        [rep_device(lax.rem(rep + step, reps)) for step in range(1, reps)]
        + [own_device(lax.rem(own + step, owns)) for step in range(1, owns)]
    )
    raw_copies = []
    for chunk in range(chunks):
        raw_copies.append([])
        for step in range(1, reps):
            target = lax.rem(rep + step, reps)
            raw_copies[-1].append(
                send(
                    gradients_ref.at[:, target * chunks + chunk],
                    raw[chunk].at[step],
                    raw_send.at[chunk, step],
                    raw_recv.at[chunk, step],
                    rep_device(target),
                )
            )
    slots = [slot_of(owner_ref, block, capacity) for block in range(block_count)]

    def source(slot):
        found = jnp.int32(0)
        for block in range(block_count):
            found = found + jnp.where(slots[block] == slot, block, 0)
        return found

    loads[0].wait()
    loads[1].wait()
    squares = [parts(dot(roots[chain], roots[chain])) for chain in chains]
    for chain in chains:
        fourth[chain] = multiply(squares[chain], squares[chain])

    own_copies = []
    for chunk in range(chunks):
        mine[chunk].wait()
        for copy in raw_copies[chunk]:
            copy.wait()
        own_copies.append([])
        for step in [*range(1, owns), 0]:
            target = lax.rem(own + step, owns)
            for place in range(capacity):
                block = source(target * capacity + place)
                value = raw[chunk][0, block].astype(jnp.float32)
                for peer in range(1, reps):
                    value = value + raw[chunk][peer, block].astype(jnp.float32)
                partial[chunk, step, place] = value
            if step:
                own_copies[-1].append(
                    send(
                        partial.at[chunk, step],
                        arrived.at[chunk, step],
                        own_send.at[chunk, step],
                        own_recv.at[chunk, step],
                        own_device(target),
                    )
                )

    high = lax.div(rep, 2)
    low = lax.rem(rep, 2)
    partner = rep_device(rep + 1 - 2 * low)
    first = []
    second = []
    for chunk in range(chunks):
        for copy in own_copies[chunk]:
            copy.wait()
        value = partial[chunk, 0]
        for step in range(1, owns):
            value = value + arrived[chunk, step]
        same[chunk, 0] = value
        first.append([])
        for step in range(1, half):
            target = lax.rem(high + step, half) * 2 + low
            first[-1].append(
                send(
                    same.at[chunk, 0],
                    same.at[chunk, step],
                    same_send.at[chunk, step],
                    same_recv.at[chunk, step],
                    rep_device(target),
                )
            )
        second.append(
            [
                send(
                    same.at[chunk, 0],
                    other.at[chunk, 0],
                    other_send.at[chunk, 0],
                    other_recv.at[chunk, 0],
                    partner,
                )
            ]
        )
    for chunk in range(chunks):
        for step in range(1, half):
            first[chunk][step - 1].wait_recv()
            second[chunk].append(
                send(
                    same.at[chunk, step],
                    other.at[chunk, step],
                    other_send.at[chunk, step],
                    other_recv.at[chunk, step],
                    partner,
                )
            )
    for copy in loads[2:]:
        copy.wait()
    for chunk in range(chunks):
        for step in range(half):
            origin = lax.rem(high + half - step, half) * 2
            second[chunk][step].wait_recv()
            for peer, held in ((origin + low, same), (origin + 1 - low, other)):
                start = pl.multiple_of(peer * row_count + chunk * piece_rows, piece_rows)
                summed[:, pl.ds(start, piece_rows), :] = held[chunk, step]

    scale = (1.0 - stat_decay) / block_size
    occupied = []
    for place in range(capacity):
        count = jnp.int32(0)
        for block in range(block_count):
            count = count + jnp.where(slots[block] == own * capacity + place, 1, 0)
        occupied.append(count > 0)
    adam_norms = []
    for place in range(capacity):
        gradient = summed[place]
        split = parts(gradient)
        for chain, axis in ((place, 1), (capacity + place, 0)):
            value = stat_decay * statistics[chain] + scale * multiply(split, split, axis, axis)
            upper[chain], lower[chain] = parts(value)
            statistics[chain] = jnp.where(occupied[place], value, statistics[chain])
        first_new = first_decay * first_in[place] + (1.0 - first_decay) * gradient
        second_new = second_decay * second_in[place] + (1.0 - second_decay) * gradient * gradient
        adam_step = first_new / (jnp.sqrt(second_new) + 1e-08)
        adam_norms.append(jnp.sqrt(total(adam_step * adam_step)))
        first_in[place] = jnp.where(occupied[place], first_new, first_in[place])
        second_in[place] = jnp.where(occupied[place], second_new, second_in[place])
    stores = []
    for place, (source_ref, target_ref) in enumerate(
        (
            (statistics.at[0:capacity], new_left_ref),
            (statistics.at[capacity : 2 * capacity], new_right_ref),
            (first_in, new_first_ref),
            (second_in, new_second_ref),
        )
    ):
        stores.append(pltpu.make_async_copy(source_ref, target_ref, store_sem.at[place]))
        stores[-1].start()

    def statistic(chain):
        return upper[chain], lower[chain]

    residuals = [parts(multiply(parts(fourth[chain]), statistic(chain))) for chain in chains]
    for chain in chains:
        initial = roots[chain]
        current[chain] = (
            5.0 * initial.astype(jnp.float32)
            - (dot(initial, residuals[chain][0]) + dot(initial, residuals[chain][1]))
        ) / 4.0

    def newton(iteration, carry):
        split = [parts(current[chain]) for chain in chains]
        squares = [parts(multiply(split[chain], split[chain])) for chain in chains]
        fourths = [parts(multiply(squares[chain], squares[chain])) for chain in chains]
        residuals = [parts(multiply(fourths[chain], statistic(chain))) for chain in chains]
        for chain in chains:
            current[chain] = (
                5.0 * current[chain] - multiply(split[chain], residuals[chain])
            ) / 4.0
        return carry

    lax.fori_loop(1, NEWTON, newton, 0)

    row_copies = []
    for place in range(capacity):
        gradient = summed[place]
        precond = multiply(
            parts(multiply(parts(current[place]), parts(gradient))),
            parts(current[capacity + place]),
        )
        graft = adam_norms[place] / (jnp.sqrt(total(precond * precond)) + 1e-06)
        kept[...] = precond
        rows = pl.ds(pl.multiple_of(rep * row_count, row_count), row_count)
        outgoing[place] = (
            master_in[place, rows, :] - learning_rate * graft * kept[rows, :]
        ).astype(jnp.bfloat16)
        for step in range(1, owns):
            row_copies.append(
                send(
                    outgoing.at[place],
                    gathered.at[step * capacity + place],
                    row_send.at[place, step],
                    row_recv.at[place, step],
                    own_device(lax.rem(own + step, owns)),
                )
            )
        gathered[place] = outgoing[place]
    for chunk in range(chunks):
        for copy in first[chunk] + second[chunk]:
            copy.wait_send()
    for copy in stores + row_copies:
        copy.wait()
    for block in range(block_count):
        step = lax.rem(own + owns - owner_ref[block], owns)
        place = jnp.minimum(slots[block] - owner_ref[block] * capacity, capacity - 1)
        weights_ref[block] = gathered[step * capacity + place]


def write(*refs):
    count = (len(refs) - 2) // 3
    loads = []
    stores = []
    for index in range(count):
        source_ref, target_ref, held = refs[index], refs[count + index], refs[2 * count + index]
        loads.append(pltpu.make_async_copy(source_ref, held, refs[-2].at[index]))
        stores.append(pltpu.make_async_copy(held, target_ref, refs[-1].at[index]))
        loads[-1].start()
    for load, store in zip(loads, stores):
        load.wait()
        store.start()
    for store in stores:
        store.wait()


def local(
    reps,
    owns,
    gradients,
    owner_index,
    left_stats,
    right_stats,
    left_roots,
    right_roots,
    first_moment,
    second_moment,
    master,
):
    capacity = left_stats.shape[0]
    block_size = left_stats.shape[-1]
    block_count = owner_index.shape[0]
    row_count = block_size // reps
    chunks = 2 if row_count % 32 == 0 else 1
    piece_rows = row_count // chunks
    half = reps // 2
    vmem = pl.BlockSpec(memory_space=pltpu.VMEM)
    smem = pl.BlockSpec(memory_space=pltpu.SMEM)
    hbm = pl.BlockSpec(memory_space=pltpu.HBM)
    dma = pltpu.SemaphoreType.DMA
    piece = (capacity, piece_rows, block_size)
    whole = (capacity, block_size, block_size)
    double = (2 * capacity, block_size, block_size)
    outputs = [jax.ShapeDtypeStruct(whole, jnp.float32)] * 4 + [
        jax.ShapeDtypeStruct((block_count, row_count, block_size), jnp.bfloat16)
    ]

    results = pl.pallas_call(
        functools.partial(step_kernel, reps, owns, chunks),
        out_shape=outputs,
        in_specs=[smem] + [hbm] * 8,
        out_specs=[hbm] * 4 + [vmem],
        scratch_shapes=[
            (pltpu.VMEM((reps, block_count, piece_rows, block_size), jnp.bfloat16),) * chunks,
            pltpu.VMEM((chunks, owns, *piece), jnp.float32),
            pltpu.VMEM((chunks, owns, *piece), jnp.float32),
            pltpu.VMEM((chunks, half, *piece), jnp.float32),
            pltpu.VMEM((chunks, half, *piece), jnp.float32),
            pltpu.VMEM(whole, jnp.float32),
            pltpu.VMEM(double, jnp.bfloat16),
            pltpu.VMEM(double, jnp.float32),
            pltpu.VMEM(whole, jnp.float32),
            pltpu.VMEM(whole, jnp.float32),
            pltpu.VMEM(whole, jnp.float32),
            pltpu.VMEM(double, jnp.float32),
            pltpu.VMEM(double, jnp.bfloat16),
            pltpu.VMEM(double, jnp.bfloat16),
            pltpu.VMEM(double, jnp.float32),
            pltpu.VMEM((block_size, block_size), jnp.float32),
            pltpu.VMEM((capacity, row_count, block_size), jnp.bfloat16),
            pltpu.VMEM((owns * capacity, row_count, block_size), jnp.bfloat16),
            dma((7,)),
            dma((4,)),
            dma((chunks,)),
            dma((chunks, reps)),
            dma((chunks, reps)),
            dma((chunks, owns)),
            dma((chunks, owns)),
            dma((chunks, half)),
            dma((chunks, half)),
            dma((chunks, half)),
            dma((chunks, half)),
            dma((capacity, owns)),
            dma((capacity, owns)),
        ],
        compiler_params=pltpu.CompilerParams(
            collective_id=0, has_side_effects=True, vmem_limit_bytes=247 * 2**18
        ),
        name="step",
    )(
        owner_index,
        gradients.reshape(block_count, reps * chunks, piece_rows, block_size),
        left_stats,
        right_stats,
        left_roots,
        right_roots,
        first_moment,
        second_moment,
        master,
    )
    return tuple(
        pl.pallas_call(
            write,
            out_shape=outputs,
            in_specs=[hbm] * 5,
            out_specs=[hbm] * 5,
            scratch_shapes=[pltpu.VMEM(leaf.shape, leaf.dtype) for leaf in outputs]
            + [dma((5,)), dma((5,))],
            compiler_params=pltpu.CompilerParams(vmem_limit_bytes=247 * 2**18),
            name="write",
        )(*results)
    )


def solution(mesh):
    return jax.shard_map(
        functools.partial(local, mesh.shape["rep"], mesh.shape["own"]),
        mesh=mesh,
        in_specs=(
            P("rep", "own", None, None, None),
            P(),
            P("own", None, None),
            P("own", None, None),
            P("own", None, None),
            P("own", None, None),
            P("own", None, None),
            P("own", None, None),
            P("own", None, None),
        ),
        out_specs=(
            P("own", None, None),
            P("own", None, None),
            P("own", None, None),
            P("own", None, None),
            P(None, "rep", None),
        ),
        check_vma=False,
    )
```

time: 161 us -> 40.5 us (0.25)
  waiting for transfers between devices: 101 us -> 0 us
  Pallas kernels: 0 us -> 39.7 us
  matrix products: 25 us -> 0 us
  between operations: 14.3 us -> 0.64 us
  blocking collectives: 13.3 us -> 0 us
  other arithmetic: 4.32 us -> 0 us
  local copies, waits for them, and re-layouts: 2.7 us -> 0 us
    psum x1 -> x0, waiting for transfers between devices: 56 us -> none  [local(): summed = lax.psum(owned_partial, 'rep')]
    reduce_scatter x1 -> x0, waiting for transfers between devices: 45.3 us -> none  [local(): lax.psum_scatter(slot_terms, 'own', scatter_dimension=0, tiled=True)]
    pallas_call x0 -> x2, Pallas kernels: none -> 39.7 us  [the longest x1 37.3 us: local(): pl.pallas_call(functools.partial(step_kernel, reps, owns, chunks), out_sh...]
    dot_general x20 -> x0, matrix products: 25 us -> none  [product(): jnp.matmul(first_factor, second_factor, precision=lax.Precision.HIGHEST)]
    all_gather x1 -> x0, blocking collectives: 13.3 us -> none  [local(): gathered = lax.all_gather(row_piece, 'own', axis=0, tiled=True)]
    select_n x3 -> x0, other arithmetic: 2.28 us -> none  [the longest x1 1.61 us: local(): jnp.where(occupied[:, None, None], local_blocks[source_block].astype(jnp....]
    gather x2 -> x0, local copies, waits for them, and re-layouts: 1.79 us -> none  [the longest x1 1.18 us: local(): weights = gathered[destination]]
  transfers between devices with their start and end apart: 2 -> 0, of which waited for: 2 -> 0; matrix products, arithmetic and copies ran while one was open for 1% -> 0% of each run, Pallas kernels for 0% -> 0%
where the time goes in v2:
time: 40.5 us; the launch traced here: 40.4 us
  Pallas kernels  39.7 us (98%)
  between operations  0.64 us (2%)
    pallas_call x1, Pallas kernels, local(): pl.pallas_call(functools.partial(step_kernel, reps, owns, chunks), out_sh...  37.3 us
    pallas_call x1, Pallas kernels, local(): pl.pallas_call(write, out_shape=outputs, in_specs=[hbm] * 5, out_specs=[h...  2.45 us

profile of v2, /device:TPU:0, one launch (start us, length us, event | category | flops | bytes accessed | tf_op | source)
XLA Modules:
  0.0 40.4 jit_solution(184343729048730)
XLA Ops:
  0.6 37.3 %step.1 = (f32[2,256,256]{2,1,0:T(8,128)}, f32[2,256,256]{2,1,0:T(8,128)}, f32[2,256,256]{2,1,0:T(8,128)}, f32[2,256,256]{2,1,0:T(8,128)}, bf16[4,32,256]{2,1,0:T(8,128)(2,1)}) custom-call(s32[4]{0:T(128)} %owner_ref.1, bf16[4,16,16,256]{3,2,1,0:T(8,128)(2,1)} %bitcast.1, f32[2,256,256]{2,1,0:T(8,128)} %left_ref.1, f32[2,256,256]{2,1,0:T(8,128)} %right_ref.1, ...), custom_call_target="tpu_custom_call" | custom-call | tf_op jit(solution)/shard_map/step/pallas_call | solution.py:415
  37.9 2.4 %write.1 = (f32[2,256,256]{2,1,0:T(8,128)}, f32[2,256,256]{2,1,0:T(8,128)}, f32[2,256,256]{2,1,0:T(8,128)}, f32[2,256,256]{2,1,0:T(8,128)}, bf16[4,32,256]{2,1,0:T(8,128)(2,1)}) custom-call(f32[2,256,256]{2,1,0:T(8,128)} %get-tuple-element.10.refs_0_, f32[2,256,256]{2,1,0:T(8,128)} %get-tuple-element.11.refs_1_, f32[2,256,256]{2,1,0:T(8,128)} %get-tuple-element.12.refs_2_, ...), custom_call_target="tpu_custom_call" | custom-call | tf_op jit(solution)/shard_map/write/pallas_call | solution.py:469

commit v3 on v2

--- a/solution.py
+++ b/solution.py
@@ -120,6 +120,8 @@
     other_recv,
     row_send,
     row_recv,
+    swap_send,
+    swap_recv,
 ):
     rep = lax.axis_index("rep")
     own = lax.axis_index("own")
@@ -129,13 +131,20 @@
     row_count = weights_ref.shape[1]
     piece_rows = row_count // chunks
     half = reps // 2
-    chains = range(2 * capacity)
+    places = range(capacity)
+    high = lax.div(rep, 2)
+    low = lax.rem(rep, 2)
 
     def rep_device(target):
         return (target, own)
 
     def own_device(target):
         return (rep, target)
+
+    partner = rep_device(rep + 1 - 2 * low)
+
+    def chain(place):
+        return low * capacity + place
 
     loads = []
     for place, (source_ref, target_ref) in enumerate(
@@ -187,9 +196,9 @@
 
     loads[0].wait()
     loads[1].wait()
-    squares = [parts(dot(roots[chain], roots[chain])) for chain in chains]
-    for chain in chains:
-        fourth[chain] = multiply(squares[chain], squares[chain])
+    squares = [parts(dot(roots[chain(place)], roots[chain(place)])) for place in places]
+    for place in places:
+        fourth[place] = multiply(squares[place], squares[place])
 
     own_copies = []
     for chunk in range(chunks):
@@ -216,9 +225,6 @@
                     )
                 )
 
-    high = lax.div(rep, 2)
-    low = lax.rem(rep, 2)
-    partner = rep_device(rep + 1 - 2 * low)
     first = []
     second = []
     for chunk in range(chunks):
@@ -280,61 +286,109 @@
         for block in range(block_count):
             count = count + jnp.where(slots[block] == own * capacity + place, 1, 0)
         occupied.append(count > 0)
+
+    stores = [
+        pltpu.make_async_copy(source_ref, target_ref, store_sem.at[place])
+        for place, (source_ref, target_ref) in enumerate(
+            (
+                (statistics.at[0:capacity], new_left_ref),
+                (statistics.at[capacity : 2 * capacity], new_right_ref),
+                (first_in, new_first_ref),
+                (second_in, new_second_ref),
+            )
+        )
+    ]
+
+    def left_statistic(place):
+        split = parts(summed[place])
+        return stat_decay * statistics[place] + scale * multiply(split, split, 1, 1)
+
+    def right_statistic(place):
+        split = parts(summed[place])
+        return stat_decay * statistics[capacity + place] + scale * multiply(split, split, 0, 0)
+
+    @pl.when(low == 0)
+    def _():
+        for place in places:
+            value = left_statistic(place)
+            upper[place], lower[place] = parts(value)
+            statistics[place] = jnp.where(occupied[place], value, statistics[place])
+
+    @pl.when(low == 1)
+    def _():
+        for place in places:
+            value = right_statistic(place)
+            upper[place], lower[place] = parts(value)
+            statistics[capacity + place] = jnp.where(
+                occupied[place], value, statistics[capacity + place]
+            )
+
+    def statistic(place):
+        return upper[place], lower[place]
+
+    residuals = [parts(multiply(parts(fourth[place]), statistic(place))) for place in places]
+    for place in places:
+        initial = roots[chain(place)]
+        current[chain(place)] = (
+            5.0 * initial.astype(jnp.float32)
+            - (dot(initial, residuals[place][0]) + dot(initial, residuals[place][1]))
+        ) / 4.0
+
+    def newton(iteration, carry):
+        split = [parts(current[chain(place)]) for place in places]
+        squares = [parts(multiply(split[place], split[place])) for place in places]
+        fourths = [parts(multiply(squares[place], squares[place])) for place in places]
+        residuals = [parts(multiply(fourths[place], statistic(place))) for place in places]
+        for place in places:
+            current[chain(place)] = (
+                5.0 * current[chain(place)] - multiply(split[place], residuals[place])
+            ) / 4.0
+        return carry
+
+    lax.fori_loop(1, NEWTON, newton, 0)
+
+    swaps = [
+        send(
+            current.at[chain(place)],
+            current.at[chain(place)],
+            swap_send.at[place],
+            swap_recv.at[place],
+            partner,
+        )
+        for place in places
+    ]
+
+    @pl.when(low == 1)
+    def _():
+        for place in places:
+            statistics[place] = jnp.where(
+                occupied[place], left_statistic(place), statistics[place]
+            )
+
+    @pl.when(low == 0)
+    def _():
+        for place in places:
+            statistics[capacity + place] = jnp.where(
+                occupied[place], right_statistic(place), statistics[capacity + place]
+            )
+
     adam_norms = []
-    for place in range(capacity):
+    for place in places:
         gradient = summed[place]
-        split = parts(gradient)
-        for chain, axis in ((place, 1), (capacity + place, 0)):
-            value = stat_decay * statistics[chain] + scale * multiply(split, split, axis, axis)
-            upper[chain], lower[chain] = parts(value)
-            statistics[chain] = jnp.where(occupied[place], value, statistics[chain])
         first_new = first_decay * first_in[place] + (1.0 - first_decay) * gradient
         second_new = second_decay * second_in[place] + (1.0 - second_decay) * gradient * gradient
         adam_step = first_new / (jnp.sqrt(second_new) + 1e-08)
         adam_norms.append(jnp.sqrt(total(adam_step * adam_step)))
         first_in[place] = jnp.where(occupied[place], first_new, first_in[place])
         second_in[place] = jnp.where(occupied[place], second_new, second_in[place])
-    stores = []
-    for place, (source_ref, target_ref) in enumerate(
-        (
-            (statistics.at[0:capacity], new_left_ref),
-            (statistics.at[capacity : 2 * capacity], new_right_ref),
-            (first_in, new_first_ref),
-            (second_in, new_second_ref),
-        )
-    ):
-        stores.append(pltpu.make_async_copy(source_ref, target_ref, store_sem.at[place]))
-        stores[-1].start()
-
-    def statistic(chain):
-        return upper[chain], lower[chain]
-
-    residuals = [parts(multiply(parts(fourth[chain]), statistic(chain))) for chain in chains]
-    for chain in chains:
-        initial = roots[chain]
-        current[chain] = (
-            5.0 * initial.astype(jnp.float32)
-            - (dot(initial, residuals[chain][0]) + dot(initial, residuals[chain][1]))
-        ) / 4.0
-
-    def newton(iteration, carry):
-        split = [parts(current[chain]) for chain in chains]
-        squares = [parts(multiply(split[chain], split[chain])) for chain in chains]
-        fourths = [parts(multiply(squares[chain], squares[chain])) for chain in chains]
-        residuals = [parts(multiply(fourths[chain], statistic(chain))) for chain in chains]
-        for chain in chains:
-            current[chain] = (
-                5.0 * current[chain] - multiply(split[chain], residuals[chain])
-            ) / 4.0
-        return carry
-
-    lax.fori_loop(1, NEWTON, newton, 0)
+    for store in stores:
+        store.start()
 
     row_copies = []
     for place in range(capacity):
-        gradient = summed[place]
+        swaps[place].wait()
         precond = multiply(
-            parts(multiply(parts(current[place]), parts(gradient))),
+            parts(multiply(parts(current[place]), parts(summed[place]))),
             parts(current[capacity + place]),
         )
         graft = adam_norms[place] / (jnp.sqrt(total(precond * precond)) + 1e-06)
@@ -398,7 +452,7 @@
     block_size = left_stats.shape[-1]
     block_count = owner_index.shape[0]
     row_count = block_size // reps
-    chunks = 2 if row_count % 32 == 0 else 1
+    chunks = 4 if row_count % 32 == 0 else 1
     piece_rows = row_count // chunks
     half = reps // 2
     vmem = pl.BlockSpec(memory_space=pltpu.VMEM)
@@ -429,9 +483,9 @@
             pltpu.VMEM(whole, jnp.float32),
             pltpu.VMEM(whole, jnp.float32),
             pltpu.VMEM(whole, jnp.float32),
-            pltpu.VMEM(double, jnp.float32),
-            pltpu.VMEM(double, jnp.bfloat16),
-            pltpu.VMEM(double, jnp.bfloat16),
+            pltpu.VMEM(whole, jnp.float32),
+            pltpu.VMEM(whole, jnp.bfloat16),
+            pltpu.VMEM(whole, jnp.bfloat16),
             pltpu.VMEM(double, jnp.float32),
             pltpu.VMEM((block_size, block_size), jnp.float32),
             pltpu.VMEM((capacity, row_count, block_size), jnp.bfloat16),
@@ -449,6 +503,8 @@
             dma((chunks, half)),
             dma((capacity, owns)),
             dma((capacity, owns)),
+            dma((capacity,)),
+            dma((capacity,)),
         ],
         compiler_params=pltpu.CompilerParams(
             collective_id=0, has_side_effects=True, vmem_limit_bytes=247 * 2**18

time: 40.5 us -> 40.5 us (level)
  no operation moved by 1% of the time
where the time goes in v3:
time: 40.5 us; the launch traced here: 40.3 us
  Pallas kernels  39.7 us (98%)
  between operations  0.64 us (2%)
    pallas_call x1, Pallas kernels, local(): pl.pallas_call(functools.partial(step_kernel, reps, owns, chunks), out_sh...  37.2 us
    pallas_call x1, Pallas kernels, local(): pl.pallas_call(write, out_shape=outputs, in_specs=[hbm] * 5, out_specs=[h...  2.45 us

profile of v3, /device:TPU:0, one launch (start us, length us, event | category | flops | bytes accessed | tf_op | source)
XLA Modules:
  0.0 40.3 jit_solution(14595600998492291834)
XLA Ops:
  0.6 37.2 %step.1 = (f32[2,256,256]{2,1,0:T(8,128)}, f32[2,256,256]{2,1,0:T(8,128)}, f32[2,256,256]{2,1,0:T(8,128)}, f32[2,256,256]{2,1,0:T(8,128)}, bf16[4,32,256]{2,1,0:T(8,128)(2,1)}) custom-call(s32[4]{0:T(128)} %owner_ref.1, bf16[4,32,8,256]{3,2,1,0:T(8,128)(2,1)} %bitcast.1, f32[2,256,256]{2,1,0:T(8,128)} %left_ref.1, f32[2,256,256]{2,1,0:T(8,128)} %right_ref.1, ...), custom_call_target="tpu_custom_call" | custom-call | tf_op jit(solution)/shard_map/step/pallas_call | solution.py:469
  37.8 2.4 %write.1 = (f32[2,256,256]{2,1,0:T(8,128)}, f32[2,256,256]{2,1,0:T(8,128)}, f32[2,256,256]{2,1,0:T(8,128)}, f32[2,256,256]{2,1,0:T(8,128)}, bf16[4,32,256]{2,1,0:T(8,128)(2,1)}) custom-call(f32[2,256,256]{2,1,0:T(8,128)} %get-tuple-element.10.refs_0_, f32[2,256,256]{2,1,0:T(8,128)} %get-tuple-element.11.refs_1_, f32[2,256,256]{2,1,0:T(8,128)} %get-tuple-element.12.refs_2_, ...), custom_call_target="tpu_custom_call" | custom-call | tf_op jit(solution)/shard_map/write/pallas_call | solution.py:525

commit v4 on v3

--- a/solution.py
+++ b/solution.py
@@ -347,6 +347,11 @@
 
     lax.fori_loop(1, NEWTON, newton, 0)
 
+    @pl.when(low == 0)
+    def _():
+        for place in places:
+            current[place] = multiply(parts(current[place]), parts(summed[place]))
+
     swaps = [
         send(
             current.at[chain(place)],
@@ -387,10 +392,7 @@
     row_copies = []
     for place in range(capacity):
         swaps[place].wait()
-        precond = multiply(
-            parts(multiply(parts(current[place]), parts(summed[place]))),
-            parts(current[capacity + place]),
-        )
+        precond = multiply(parts(current[place]), parts(current[capacity + place]))
         graft = adam_norms[place] / (jnp.sqrt(total(precond * precond)) + 1e-06)
         kept[...] = precond
         rows = pl.ds(pl.multiple_of(rep * row_count, row_count), row_count)
@@ -425,9 +427,14 @@
     stores = []
     for index in range(count):
         source_ref, target_ref, held = refs[index], refs[count + index], refs[2 * count + index]
-        loads.append(pltpu.make_async_copy(source_ref, held, refs[-2].at[index]))
-        stores.append(pltpu.make_async_copy(held, target_ref, refs[-1].at[index]))
-        loads[-1].start()
+        for part in range(source_ref.shape[0]):
+            loads.append(
+                pltpu.make_async_copy(source_ref.at[part], held.at[part], refs[-2].at[index, part])
+            )
+            stores.append(
+                pltpu.make_async_copy(held.at[part], target_ref.at[part], refs[-1].at[index, part])
+            )
+            loads[-1].start()
     for load, store in zip(loads, stores):
         load.wait()
         store.start()
@@ -528,7 +535,7 @@
             in_specs=[hbm] * 5,
             out_specs=[hbm] * 5,
             scratch_shapes=[pltpu.VMEM(leaf.shape, leaf.dtype) for leaf in outputs]
-            + [dma((5,)), dma((5,))],
+            + [dma((5, max(capacity, block_count)))] * 2,
             compiler_params=pltpu.CompilerParams(vmem_limit_bytes=247 * 2**18),
             name="write",
         )(*results)

time: 40.5 us -> 40.3 us (level)
  no operation moved by 1% of the time
where the time goes in v4:
time: 40.3 us; the launch traced here: 40.2 us
  Pallas kernels  39.5 us (98%)
  between operations  0.64 us (2%)
    pallas_call x1, Pallas kernels, local(): pl.pallas_call(functools.partial(step_kernel, reps, owns, chunks), out_sh...  36.9 us
    pallas_call x1, Pallas kernels, local(): pl.pallas_call(write, out_shape=outputs, in_specs=[hbm] * 5, out_specs=[h...  2.62 us

profile of v4, /device:TPU:0, one launch (start us, length us, event | category | flops | bytes accessed | tf_op | source)
XLA Modules:
  0.0 40.2 jit_solution(10941602286323940966)
XLA Ops:
  0.6 36.9 %step.1 = (f32[2,256,256]{2,1,0:T(8,128)}, f32[2,256,256]{2,1,0:T(8,128)}, f32[2,256,256]{2,1,0:T(8,128)}, f32[2,256,256]{2,1,0:T(8,128)}, bf16[4,32,256]{2,1,0:T(8,128)(2,1)}) custom-call(s32[4]{0:T(128)} %owner_ref.1, bf16[4,32,8,256]{3,2,1,0:T(8,128)(2,1)} %bitcast.1, f32[2,256,256]{2,1,0:T(8,128)} %left_ref.1, f32[2,256,256]{2,1,0:T(8,128)} %right_ref.1, ...), custom_call_target="tpu_custom_call" | custom-call | tf_op jit(solution)/shard_map/step/pallas_call | solution.py:476
  37.6 2.6 %write.1 = (f32[2,256,256]{2,1,0:T(8,128)}, f32[2,256,256]{2,1,0:T(8,128)}, f32[2,256,256]{2,1,0:T(8,128)}, f32[2,256,256]{2,1,0:T(8,128)}, bf16[4,32,256]{2,1,0:T(8,128)(2,1)}) custom-call(f32[2,256,256]{2,1,0:T(8,128)} %get-tuple-element.10.refs_0_, f32[2,256,256]{2,1,0:T(8,128)} %get-tuple-element.11.refs_1_, f32[2,256,256]{2,1,0:T(8,128)} %get-tuple-element.12.refs_2_, ...), custom_call_target="tpu_custom_call" | custom-call | tf_op jit(solution)/shard_map/write/pallas_call | solution.py:532
